TPU v7x, 512 devices: a whole 4x4x16 slice. The times are simulated.
512 devices in a mesh: wide: 64 (over x, z), narrow: 8 (over y, core).
Axes of the slice: x: 4, y: 4, z: 16, core: 2. Of those that a mesh axis runs over, the one named last changes fastest.
Arguments:
- frames: bfloat16 [16384, 1024], P('wide'), may hold values from -6 to 6
- expert_ids: int32 [16384, 2], P('wide'), may hold values from 0 to 63, all different within a row; in each aligned block of 256 rows (0 to 255, 256 to 511, ...) at most 16 rows name the same one
- gate_values: float32 [16384, 2], P('wide'), may hold values from 0.1 to 1
- w_gate: bfloat16 [64, 1024, 4096], P('wide', None, 'narrow'), may hold values from -0.1875 to 0.1875
- w_up: bfloat16 [64, 1024, 4096], P('wide', None, 'narrow'), may hold values from -0.1875 to 0.1875
- w_down: bfloat16 [64, 4096, 1024], P('wide', 'narrow'), may hold values from -0.09375 to 0.09375
- norm_gain: float32 [1024], replicated, may hold values from 0.1 to 1.9
- norm_bias: float32 [1024], replicated, may hold values from -2 to 2
- point_in: bfloat16 [1024, 2, 1024], P(None, None, 'narrow'), may hold values from -0.1875 to 0.1875
- depth_kernel: bfloat16 [31, 1024], P(None, 'narrow'), may hold values from -1 to 1
- point_out: bfloat16 [1024, 1024], P('narrow'), may hold values from -0.1875 to 0.1875
Outputs:
- block_out: bfloat16 [16384, 1024], P(('wide', 'narrow'))
Inputs may be any that keep to these rules, and one draw needn't show every extreme that they name: `expert_ids`: each frame names 2 different experts; in each aligned block of 256 frames no expert is named by more than 16 frames, and every expert is named somewhere.
All inputs are finite; a program needn't handle non-finite values.
Results may differ from a plain program's by a relative error of at most 0.015.
Values may be sent and summed in bfloat16 or wider, within the bound.
No kernel may reach another device: no remote copies, remote signals or barrier semaphores. Data moves between devices by JAX's collectives and lax.ppermute only.
A program may use at most 64 MiB of HBM per device.

v0:
```python
import jax
import jax.numpy as jnp
from jax import lax
from jax.sharding import PartitionSpec as P


def padded_2(cells, sides, width):
    for axis, dim in sides:
        count = lax.axis_size(axis)
        ends = count - 1
        head = lax.slice_in_dim(cells, 0, width, axis=dim)
        tail = lax.slice_in_dim(cells, cells.shape[dim] - width, cells.shape[dim], axis=dim)
        cells = jnp.concatenate(
            [
                lax.ppermute(tail, axis, [(i, (i + 1) % count) for i in range(ends)]),
                cells,
                lax.ppermute(head, axis, [((i + 1) % count, i) for i in range(ends)]),
            ],
            axis=dim,
        )
    return cells


def shards(
    frames,
    expert_ids,
    gate_values,
    w_gate,
    w_up,
    w_down,
    norm_gain,
    norm_bias,
    point_in,
    depth_kernel,
    point_out,
):
    frame_count = frames.shape[0]
    model_width = frames.shape[1]
    top_count = expert_ids.shape[1]
    wide_count = lax.axis_size("wide")
    narrow_count = lax.axis_size("narrow")
    local_experts = w_gate.shape[0]
    expert_count = local_experts * wide_count
    capacity = 2 * top_count * frame_count // expert_count
    flat_ids = expert_ids.reshape(-1)
    one_hot = (flat_ids[:, None] == jnp.arange(expert_count, dtype=jnp.int32)[None, :]).astype(
        jnp.int32
    )
    running = jnp.cumsum(one_hot, axis=0)
    slot_index = jnp.sum((running - 1) * one_hot, axis=1)
    target_row = flat_ids * capacity + slot_index
    repeated = jnp.repeat(frames, top_count, axis=0)
    outgoing = (
        jnp.zeros((expert_count * capacity, model_width), jnp.bfloat16).at[target_row].set(repeated)
    )
    outgoing = outgoing.reshape(expert_count, capacity, model_width)
    arrived = lax.all_to_all(outgoing, "wide", split_axis=0, concat_axis=0, tiled=True)
    arrived = arrived.reshape(wide_count, local_experts, capacity, model_width)
    gate_h = jnp.einsum("sjcd,jdf->sjcf", arrived, w_gate, preferred_element_type=jnp.float32)
    up_h = jnp.einsum("sjcd,jdf->sjcf", arrived, w_up, preferred_element_type=jnp.float32)
    hidden = (jax.nn.silu(gate_h) * up_h).astype(jnp.bfloat16)
    partial_value = jnp.einsum(
        "sjcf,jfd->sjcd", hidden, w_down, preferred_element_type=jnp.float32
    ).astype(jnp.bfloat16)
    partial_value = partial_value.reshape(wide_count * local_experts, capacity, model_width)
    returned = lax.all_to_all(partial_value, "wide", split_axis=0, concat_axis=0, tiled=True)
    picked = jnp.take(returned.reshape(expert_count * capacity, model_width), target_row, axis=0)
    picked = picked.reshape(frame_count, top_count, model_width)
    mixture = jnp.sum(gate_values[:, :, None] * picked.astype(jnp.float32), axis=1)
    moe_sum = lax.psum(mixture.astype(jnp.bfloat16), "narrow").astype(jnp.float32)
    residual = frames.astype(jnp.float32) + moe_sum
    row_mean = jnp.mean(residual, axis=1, keepdims=True)
    centered = residual - row_mean
    row_var = jnp.mean(centered * centered, axis=1, keepdims=True)
    normed = (
        centered / jnp.sqrt(row_var + 1e-05) * norm_gain[None, :] + norm_bias[None, :]
    ).astype(jnp.bfloat16)
    channels = point_in.shape[2]
    projected = jnp.dot(
        normed, point_in.reshape(model_width, 2 * channels), preferred_element_type=jnp.float32
    )
    value_half = projected[:, :channels]
    gate_half = projected[:, channels:]
    glu_out = (value_half * jax.nn.sigmoid(gate_half)).astype(jnp.bfloat16)
    taps_count = depth_kernel.shape[0]
    half_width = (taps_count - 1) // 2
    padded = padded_2(glu_out, (("wide", 0),), half_width)
    depthwise = jnp.zeros((frame_count, channels), jnp.float32)
    for tap_index in range(taps_count):
        depthwise = (
            depthwise
            + padded[tap_index : tap_index + frame_count].astype(jnp.float32)
            * depth_kernel[tap_index].astype(jnp.float32)[None, :]
        )
    activated = (depthwise * jax.nn.sigmoid(depthwise)).astype(jnp.bfloat16)
    share_rows = frame_count // narrow_count
    summed = lax.psum_scatter(
        jnp.dot(activated, point_out, preferred_element_type=jnp.float32).astype(jnp.bfloat16),
        "narrow",
        scatter_dimension=0,
        tiled=True,
    ).astype(jnp.float32)
    own_rows = lax.dynamic_slice_in_dim(
        residual, lax.axis_index("narrow") * share_rows, share_rows, 0
    )
    return (own_rows + summed).astype(jnp.bfloat16)


def solution(mesh):
    return jax.shard_map(
        shards,
        mesh=mesh,
        in_specs=(
            P("wide", None),
            P("wide", None),
            P("wide", None),
            P("wide", None, "narrow"),
            P("wide", None, "narrow"),
            P("wide", "narrow", None),
            P(),
            P(),
            P(None, None, "narrow"),
            P(None, "narrow"),
            P("narrow", None),
        ),
        out_specs=P(("wide", "narrow"), None),
        check_vma=False,
    )
```

profile of v0, /device:TPU:2, one launch (start us, length us, event | category | flops | bytes accessed | tf_op | source)
XLA Modules:
  0.0 387.4 jit_solution(1770547481121458651)
XLA Ops:
  6.5 0.9 copy.20
  7.7 0.7 broadcast_multiply_fusion
  8.4 1.2 reduce-window.6
  10.2 1.6 broadcast_in_dim.16
  11.8 1.2 reshape.166
  13.2 3.9 %scatter_custom_fusion = bf16[1024,1024]{1,0:T(8,128)(2,1)S(1)} fusion(s32[512]{0:T(512)S(1)} %bitcast.172, bf16[512,1024]{1,0:T(8,128)(2,1)} %reshape.166, bf16[]{:T(256)} %constant.21.clone.1), kind=kCustom, calls=%fused_computation.22 | custom fusion | bytes 2097664 | tf_op jit(solution)/shard_map/scatter | solution.py:54
  17.1 116.1 %all_to_all.10 = bf16[64,16,1024]{2,1,0:T(8,128)(2,1)S(1)} all-to-all(bf16[64,16,1024]{2,1,0:T(8,128)(2,1)S(1)} %bitcast.170), channel_id=1, replica_groups=mesh['wide'=64,'narrow'=8] {'wide'}, dimensions={0} | all-to-all | bytes 4194304 | tf_op jit(solution)/shard_map/all_to_all | solution.py:57
  133.2 1.3 copy-done.2
  134.5 2.5 fusion.8
  137.1 6.0 %convolution_convert_fusion = bf16[64,16,1024]{2,1,0:T(8,128)(2,1)} fusion(bf16[64,16,1024]{2,1,0:T(8,128)(2,1)} %copy-done.2, f32[64,16,512]{2,1,0:T(8,128)} %fusion.8, bf16[1,512,1024]{2,1,0:T(8,128)(2,1)S(1)} %copy-done, bf16[1,1024,512]{2,1,0:T(8,128)(2,1)S(1)} %copy-done.8), kind=kOutput, calls=%fused_computation.11 | convolution fusion | flops 2151677952 | bytes 8388608 | tf_op jit(solution)/shard_map/sjcf,jfd->sjcd/dot_general | solution.py:62
  143.1 8.2 %all-to-all-start.1 = ((bf16[64,16,1024]{2,1,0:T(8,128)(2,1)}), bf16[64,16,1024]{2,1,0:T(8,128)(2,1)S(1)}, u32[]{:S(2)}, u32[]{:S(2)}) async-start(bf16[64,16,1024]{2,1,0:T(8,128)(2,1)} %convolution_convert_fusion), calls=%async_computation.1 | async-start | bytes 4194304 | tf_op jit(solution)/shard_map/all_to_all | solution.py:66
  152.1 96.1 %all-to-all-done.1 = bf16[64,16,1024]{2,1,0:T(8,128)(2,1)S(1)} async-done(((bf16[64,16,1024]{2,1,0:T(8,128)(2,1)}), bf16[64,16,1024]{2,1,0:T(8,128)(2,1)S(1)}, u32[]{:S(2)}, u32[]{:S(2)}) %all-to-all-start.1) | async-done | bytes 2097184 | tf_op jit(solution)/shard_map/all_to_all | solution.py:66
  248.2 2.8 gather_fusion
  251.0 1.5 gather.7
  252.6 5.0 %multiply_reduce_fusion = bf16[256,1024]{1,0:T(8,128)(2,1)} fusion(bf16[256,2,1024]{2,1,0:T(2,128)(2,1)S(1)} %gather.7, pred[256,2]{1,0:T(8,128)(4,1)S(1)} %copy.24, f32[256,2]{1,0:T(8,128)S(1)} %copy.19), kind=kLoop, calls=%fused_computation.9 | loop fusion | flops 1835008 | bytes 1575424 | tf_op jit(solution)/shard_map/reduce_sum | solution.py:69
  257.7 70.7 %all-reduce.2.cloned.1.call-done = bf16[256,1024]{1,0:T(8,128)(2,1)} async-done(((bf16[256,1024]{1,0:T(8,128)(2,1)}), bf16[256,1024]{1,0:T(8,128)(2,1)}) %all-reduce.2.cloned.1.call-update) | async-done | bytes 524304 | tf_op jit(solution)/shard_map/psum | solution.py:70
  328.5 1.3 convert_add_fusion
  330.2 0.5 fusion.13
  330.7 3.5 collective-permute-start
  334.2 4.5 %collective-permute-start.1 = (bf16[15,128]{1,0:T(8,128)(2,1)S(1)}, bf16[15,128]{1,0:T(8,128)(2,1)S(1)}, u32[]{:S(2)}, u32[]{:S(2)}) collective-permute-start(bf16[15,128]{1,0:T(8,128)(2,1)S(1)} %get-tuple-element.8), channel_id=1, source_target_pairs={{8,0},{16,8},{24,16},{32,24},{40,32},{48,40},{56,48},{64,56},{72,6... | collective-permute-start | bytes 11528 | tf_op jit(solution)/shard_map/ppermute | solution.py:17
  338.7 1.3 collective-permute-done.1
  340.0 1.5 convolution_convert_fusion.1
  341.5 37.6 %reduce-scatter.2.cloned.1.call-done = bf16[32,1024]{1,0:T(8,128)(2,1)} async-done(((bf16[256,1024]{1,0:T(8,128)(2,1)}), bf16[32,1024]{1,0:T(8,128)(2,1)}) %reduce-scatter.2.cloned.1.call-update) | async-done | bytes 65552 | tf_op jit(solution)/shard_map/reduce_scatter | solution.py:97
  379.1 1.5 add_convert_fusion.2
  (53 shorter events, 2.3 us)
Async XLA Ops:
  6.5 130.5 %copy-start = (bf16[1,512,1024]{2,1,0:T(8,128)(2,1)S(1)}, bf16[1,512,1024]{2,1,0:T(8,128)(2,1)}, u32[]{:S(2)}) copy-start(bf16[1,512,1024]{2,1,0:T(8,128)(2,1)} %param.16) | copy-start | bytes 3145732
  17.1 117.5 %copy-start.7 = (bf16[1,1024,512]{2,1,0:T(8,128)(2,1)S(1)}, bf16[1,1024,512]{2,1,0:T(8,128)(2,1)}, u32[]{:S(2)}) copy-start(bf16[1,1024,512]{2,1,0:T(8,128)(2,1)} %param.14) | copy-start | bytes 3145732
  133.2 1.4 copy-start.2
  134.5 2.5 copy-start.8
  143.0 8.7 %copy-start.5 = (s32[256,2]{0,1:T(2,128)S(1)}, s32[256,2]{0,1:T(2,128)}, u32[]{:S(2)}) copy-start(s32[256,2]{0,1:T(2,128)} %param.12) | copy-start | bytes 6148
  143.1 8.9 %copy-start.6 = (f32[256,2]{0,1:T(2,128)S(1)}, f32[256,2]{0,1:T(2,128)}, u32[]{:S(2)}) copy-start(f32[256,2]{0,1:T(2,128)} %param.13) | copy-start | bytes 6148
  143.1 105.2 %all-to-all-start.1 = ((bf16[64,16,1024]{2,1,0:T(8,128)(2,1)}), bf16[64,16,1024]{2,1,0:T(8,128)(2,1)S(1)}, u32[]{:S(2)}, u32[]{:S(2)}) async-start(bf16[64,16,1024]{2,1,0:T(8,128)(2,1)} %convolution_convert_fusion), calls=%async_computation.1 | async-start | bytes 4194304 | tf_op jit(solution)/shard_map/all_to_all | solution.py:66
  151.3 177.2 %all-reduce.2.cloned.1.call-start = ((), (), s32[]{:S(2)}) async-start(), calls=%async_computation.3 | async-start | bytes 1048576 | tf_op jit(solution)/shard_map/psum | solution.py:70
  251.0 6.7 %copy-start.4 = (bf16[31,128]{1,0:T(8,128)(2,1)S(1)}, bf16[31,128]{1,0:T(8,128)(2,1)}, u32[]{:S(2)}) copy-start(bf16[31,128]{1,0:T(8,128)(2,1)} %param.20) | copy-start | bytes 23812
  251.0 77.4 %copy-start.1 = (bf16[256,1024]{1,0:T(8,128)(2,1)S(1)}, bf16[256,1024]{1,0:T(8,128)(2,1)}, u32[]{:S(2)}) copy-start(bf16[256,1024]{1,0:T(8,128)(2,1)} %param.11) | copy-start | bytes 1572868
  257.6 72.5 %copy-start.9 = (bf16[1024,2,128]{2,1,0:T(2,128)(2,1)S(1)}, bf16[1024,2,128]{2,1,0:T(2,128)(2,1)}, u32[]{:S(2)}) copy-start(bf16[1024,2,128]{2,1,0:T(2,128)(2,1)} %param.19) | copy-start | bytes 1572868
  257.6 72.5 %copy-start.11 = (f32[1024]{0:T(1024)S(1)}, f32[1024]{0:T(1024)}, u32[]{:S(2)}) copy-start(f32[1024]{0:T(1024)} %param.18) | copy-start | bytes 12292
  257.6 72.5 %copy-start.12 = (f32[1024]{0:T(1024)S(1)}, f32[1024]{0:T(1024)}, u32[]{:S(2)}) copy-start(f32[1024]{0:T(1024)} %param.17) | copy-start | bytes 12292
  257.6 121.5 %reduce-scatter.2.cloned.1.call-start = ((), (), s32[]{:S(2)}) async-start(), calls=%async_computation.4 | async-start | bytes 589824 | tf_op jit(solution)/shard_map/reduce_scatter | solution.py:97
  328.5 1.3 copy-start.3
  330.1 9.8 %copy-start.10 = (bf16[128,1024]{1,0:T(8,128)(2,1)S(1)}, bf16[128,1024]{1,0:T(8,128)(2,1)}, u32[]{:S(2)}) copy-start(bf16[128,1024]{1,0:T(8,128)(2,1)} %param.21) | copy-start | bytes 786436
  330.7 8.0 %collective-permute-start = (bf16[15,128]{1,0:T(8,128)(2,1)S(1)}, bf16[15,128]{1,0:T(8,128)(2,1)S(1)}, u32[]{:S(2)}, u32[]{:S(2)}) collective-permute-start(bf16[15,128]{1,0:T(8,128)(2,1)S(1)} %get-tuple-element.7), channel_id=1, source_target_pairs={{0,8},{8,16},{16,24},{24,32},{32,40},{40,48},{48,56},{56,64},{64,7... | collective-permute-start | bytes 11528 | tf_op jit(solution)/shard_map/ppermute | solution.py:15
  334.2 5.8 %collective-permute-start.1 = (bf16[15,128]{1,0:T(8,128)(2,1)S(1)}, bf16[15,128]{1,0:T(8,128)(2,1)S(1)}, u32[]{:S(2)}, u32[]{:S(2)}) collective-permute-start(bf16[15,128]{1,0:T(8,128)(2,1)S(1)} %get-tuple-element.8), channel_id=1, source_target_pairs={{8,0},{16,8},{24,16},{32,24},{40,32},{48,40},{56,48},{64,56},{72,6... | collective-permute-start | bytes 11528 | tf_op jit(solution)/shard_map/ppermute | solution.py:17
Sparse Core Ops, SparseCore 0:
  257.8 70.6 all-reduce.1
  341.6 37.4 reduce-scatter.1
where the time goes:
time: 388 us; the launch traced here: 387 us
  waiting for transfers between devices  206 us (53%)
  blocking collectives  116 us (30%)
  starting transfers between devices  16.4 us (4%)
  local copies, waits for them, and re-layouts  14.7 us (4%)
  between operations  13.6 us (4%)
  matrix products  10.5 us (3%)
  other arithmetic  10.3 us (3%)
    all_to_all x1, blocking collectives, shards(): lax.all_to_all(outgoing, 'wide', split_axis=0, concat_axis=0, tiled=True)  116 us
    all_to_all x1, waiting for transfers between devices, shards(): lax.all_to_all(partial_value, 'wide', split_axis=0, concat_axis=0, tiled=...  96.1 us
    psum x1, waiting for transfers between devices, shards(): lax.psum(mixture.astype(jnp.bfloat16), 'narrow').astype(jnp.float32)  70.7 us
    reduce_scatter x1, waiting for transfers between devices, shards(): lax.psum_scatter(jnp.dot(activated, point_out, preferred_element_type=jnp...  37.6 us
    all_to_all x1, starting transfers between devices, shards(): lax.all_to_all(partial_value, 'wide', split_axis=0, concat_axis=0, tiled=...  8.22 us
  transfers between devices with their start and end apart: 5, of which 4 were waited for; matrix products, arithmetic and copies ran while one was open for 0% of the time, Pallas kernels for 0%

commit v1 on v0

--- a/solution.py
+++ b/solution.py
@@ -67,7 +67,9 @@
     picked = jnp.take(returned.reshape(expert_count * capacity, model_width), target_row, axis=0)
     picked = picked.reshape(frame_count, top_count, model_width)
     mixture = jnp.sum(gate_values[:, :, None] * picked.astype(jnp.float32), axis=1)
-    moe_sum = lax.psum(mixture.astype(jnp.bfloat16), "narrow").astype(jnp.float32)
+    moe_sum = jnp.sum(lax.all_gather(mixture.astype(jnp.bfloat16), "narrow"), axis=0).astype(
+        jnp.float32
+    )
     residual = frames.astype(jnp.float32) + moe_sum
     row_mean = jnp.mean(residual, axis=1, keepdims=True)
     centered = residual - row_mean

time: 388 us -> 355 us (0.915)
  waiting for transfers between devices: 206 us -> 170 us
    psum x1 -> x0, waiting for transfers between devices: 70.7 us -> none  [shards(): lax.psum(mixture.astype(jnp.bfloat16), 'narrow').astype(jnp.float32)]
    all_gather x0 -> x1, waiting for transfers between devices: none -> 34.4 us  [shards(): lax.all_gather(mixture.astype(jnp.bfloat16), 'narrow')]
where the time goes in v1:
time: 355 us
  waiting for transfers between devices  170 us (48%)
  blocking collectives  116 us (33%)
  starting transfers between devices  16.4 us (5%)
  local copies, waits for them, and re-layouts  15.1 us (4%)
  between operations  13.6 us (4%)
  other arithmetic  12.4 us (3%)
  matrix products  10.5 us (3%)
    all_to_all x1, blocking collectives, shards(): lax.all_to_all(outgoing, 'wide', split_axis=0, concat_axis=0, tiled=True)  116 us
    all_to_all x1, waiting for transfers between devices, shards(): lax.all_to_all(partial_value, 'wide', split_axis=0, concat_axis=0, tiled=...  96.1 us
    reduce_scatter x1, waiting for transfers between devices, shards(): lax.psum_scatter(jnp.dot(activated, point_out, preferred_element_type=jnp...  38.6 us
    all_gather x1, waiting for transfers between devices, shards(): lax.all_gather(mixture.astype(jnp.bfloat16), 'narrow')  34.4 us
    all_to_all x1, starting transfers between devices, shards(): lax.all_to_all(partial_value, 'wide', split_axis=0, concat_axis=0, tiled=...  8.22 us
  transfers between devices with their start and end apart: 5, of which 4 were waited for; matrix products, arithmetic and copies ran while one was open for 0% of the time, Pallas kernels for 0%

profile of v1, /device:TPU:2, one launch (start us, length us, event | category | flops | bytes accessed | tf_op | source)
XLA Modules:
  0.0 354.6 jit_solution(15997984566493390236)
XLA Ops:
  6.5 0.9 copy.25
  7.7 0.7 broadcast_multiply_fusion
  8.4 1.2 reduce-window.6
  10.2 1.6 broadcast_in_dim.16
  11.8 1.2 reshape.174
  13.2 3.9 %scatter_custom_fusion = bf16[1024,1024]{1,0:T(8,128)(2,1)S(1)} fusion(s32[512]{0:T(512)S(1)} %bitcast.174, bf16[512,1024]{1,0:T(8,128)(2,1)} %reshape.174, bf16[]{:T(256)} %constant.22.clone.1), kind=kCustom, calls=%fused_computation.22 | custom fusion | bytes 2097664 | tf_op jit(solution)/shard_map/scatter | solution.py:54
  17.1 116.1 %all_to_all.10 = bf16[64,16,1024]{2,1,0:T(8,128)(2,1)S(1)} all-to-all(bf16[64,16,1024]{2,1,0:T(8,128)(2,1)S(1)} %bitcast.171), channel_id=1, replica_groups=mesh['wide'=64,'narrow'=8] {'wide'}, dimensions={0} | all-to-all | bytes 4194304 | tf_op jit(solution)/shard_map/all_to_all | solution.py:57
  133.2 1.3 copy-done.2
  134.5 2.5 fusion.8
  137.1 6.0 %convolution_convert_fusion = bf16[64,16,1024]{2,1,0:T(8,128)(2,1)} fusion(bf16[64,16,1024]{2,1,0:T(8,128)(2,1)} %copy-done.2, f32[64,16,512]{2,1,0:T(8,128)} %fusion.8, bf16[1,512,1024]{2,1,0:T(8,128)(2,1)S(1)} %copy-done, bf16[1,1024,512]{2,1,0:T(8,128)(2,1)S(1)} %copy-done.7), kind=kOutput, calls=%fused_computation.11 | convolution fusion | flops 2151677952 | bytes 8388608 | tf_op jit(solution)/shard_map/sjcf,jfd->sjcd/dot_general | solution.py:62
  143.1 8.2 %all-to-all-start.1 = ((bf16[64,16,1024]{2,1,0:T(8,128)(2,1)}), bf16[64,16,1024]{2,1,0:T(8,128)(2,1)S(1)}, u32[]{:S(2)}, u32[]{:S(2)}) async-start(bf16[64,16,1024]{2,1,0:T(8,128)(2,1)} %convolution_convert_fusion), calls=%async_computation.1 | async-start | bytes 4194304 | tf_op jit(solution)/shard_map/all_to_all | solution.py:66
  152.1 96.1 %all-to-all-done.1 = bf16[64,16,1024]{2,1,0:T(8,128)(2,1)S(1)} async-done(((bf16[64,16,1024]{2,1,0:T(8,128)(2,1)}), bf16[64,16,1024]{2,1,0:T(8,128)(2,1)S(1)}, u32[]{:S(2)}, u32[]{:S(2)}) %all-to-all-start.1) | async-done | bytes 2097184 | tf_op jit(solution)/shard_map/all_to_all | solution.py:66
  248.2 2.8 gather_fusion
  251.0 1.5 gather.7
  252.5 5.0 %multiply_reduce_fusion = bf16[256,1024]{1,0:T(8,128)(2,1)} fusion(bf16[256,2,1024]{2,1,0:T(2,128)(2,1)S(1)} %gather.7, pred[256,2]{1,0:T(8,128)(4,1)S(1)} %copy.29, f32[256,2]{1,0:T(8,128)S(1)} %copy.24), kind=kLoop, calls=%fused_computation.9 | loop fusion | flops 1835008 | bytes 1575424 | tf_op jit(solution)/shard_map/reduce_sum | solution.py:69
  257.7 34.4 %all-gather.3.cloned.1.call-done = bf16[2048,1024]{1,0:T(8,128)(2,1)} async-done(((bf16[256,1024]{1,0:T(8,128)(2,1)}), bf16[2048,1024]{1,0:T(8,128)(2,1)}) %all-gather.3.cloned.1.call-update) | async-done | bytes 4194320 | tf_op jit(solution)/shard_map/all_gather | solution.py:70
  292.1 3.2 reduce_sum.56
  295.8 0.5 copy-done.8
  296.8 3.5 collective-permute-start
  300.3 4.5 %collective-permute-start.1 = (bf16[15,128]{1,0:T(8,128)(2,1)S(1)}, bf16[15,128]{1,0:T(8,128)(2,1)S(1)}, u32[]{:S(2)}, u32[]{:S(2)}) collective-permute-start(bf16[15,128]{1,0:T(8,128)(2,1)S(1)} %get-tuple-element.8), channel_id=1, source_target_pairs={{8,0},{16,8},{24,16},{32,24},{40,32},{48,40},{56,48},{64,56},{72,6... | collective-permute-start | bytes 11528 | tf_op jit(solution)/shard_map/ppermute | solution.py:17
  304.8 1.3 collective-permute-done.1
  306.1 1.5 convolution_convert_fusion.1
  307.6 38.6 %reduce-scatter.2.cloned.1.call-done = bf16[32,1024]{1,0:T(8,128)(2,1)} async-done(((bf16[256,1024]{1,0:T(8,128)(2,1)}), bf16[32,1024]{1,0:T(8,128)(2,1)}) %reduce-scatter.2.cloned.1.call-update) | async-done | bytes 65552 | tf_op jit(solution)/shard_map/reduce_scatter | solution.py:99
  346.3 1.5 add_convert_fusion.2
  (52 shorter events, 2.9 us)
Async XLA Ops:
  6.5 130.5 %copy-start = (bf16[1,512,1024]{2,1,0:T(8,128)(2,1)S(1)}, bf16[1,512,1024]{2,1,0:T(8,128)(2,1)}, u32[]{:S(2)}) copy-start(bf16[1,512,1024]{2,1,0:T(8,128)(2,1)} %param.16) | copy-start | bytes 3145732
  17.1 117.5 %copy-start.6 = (bf16[1,1024,512]{2,1,0:T(8,128)(2,1)S(1)}, bf16[1,1024,512]{2,1,0:T(8,128)(2,1)}, u32[]{:S(2)}) copy-start(bf16[1,1024,512]{2,1,0:T(8,128)(2,1)} %param.14) | copy-start | bytes 3145732
  133.2 1.4 copy-start.2
  134.5 2.5 copy-start.7
  143.0 8.7 %copy-start.4 = (s32[256,2]{0,1:T(2,128)S(1)}, s32[256,2]{0,1:T(2,128)}, u32[]{:S(2)}) copy-start(s32[256,2]{0,1:T(2,128)} %param.12) | copy-start | bytes 6148
  143.1 8.9 %copy-start.5 = (f32[256,2]{0,1:T(2,128)S(1)}, f32[256,2]{0,1:T(2,128)}, u32[]{:S(2)}) copy-start(f32[256,2]{0,1:T(2,128)} %param.13) | copy-start | bytes 6148
  143.1 105.2 %all-to-all-start.1 = ((bf16[64,16,1024]{2,1,0:T(8,128)(2,1)}), bf16[64,16,1024]{2,1,0:T(8,128)(2,1)S(1)}, u32[]{:S(2)}, u32[]{:S(2)}) async-start(bf16[64,16,1024]{2,1,0:T(8,128)(2,1)} %convolution_convert_fusion), calls=%async_computation.1 | async-start | bytes 4194304 | tf_op jit(solution)/shard_map/all_to_all | solution.py:66
  151.3 140.8 %all-gather.3.cloned.1.call-start = ((), (), s32[]{:S(2)}) async-start(), calls=%async_computation.4 | async-start | bytes 4718592 | tf_op jit(solution)/shard_map/all_gather | solution.py:70
  251.0 6.6 %copy-start.3 = (bf16[31,128]{1,0:T(8,128)(2,1)S(1)}, bf16[31,128]{1,0:T(8,128)(2,1)}, u32[]{:S(2)}) copy-start(bf16[31,128]{1,0:T(8,128)(2,1)} %param.20) | copy-start | bytes 23812
  257.6 88.7 %reduce-scatter.2.cloned.1.call-start = ((), (), s32[]{:S(2)}) async-start(), calls=%async_computation.3 | async-start | bytes 589824 | tf_op jit(solution)/shard_map/reduce_scatter | solution.py:99
  292.1 3.2 copy-start.1
  295.2 1.0 copy-start.8
  295.2 1.0 copy-start.10
  295.2 1.0 copy-start.11
  296.3 9.8 %copy-start.9 = (bf16[128,1024]{1,0:T(8,128)(2,1)S(1)}, bf16[128,1024]{1,0:T(8,128)(2,1)}, u32[]{:S(2)}) copy-start(bf16[128,1024]{1,0:T(8,128)(2,1)} %param.21) | copy-start | bytes 786436
  296.8 8.0 %collective-permute-start = (bf16[15,128]{1,0:T(8,128)(2,1)S(1)}, bf16[15,128]{1,0:T(8,128)(2,1)S(1)}, u32[]{:S(2)}, u32[]{:S(2)}) collective-permute-start(bf16[15,128]{1,0:T(8,128)(2,1)S(1)} %get-tuple-element.7), channel_id=1, source_target_pairs={{0,8},{8,16},{16,24},{24,32},{32,40},{40,48},{48,56},{56,64},{64,7... | collective-permute-start | bytes 11528 | tf_op jit(solution)/shard_map/ppermute | solution.py:15
  300.3 5.8 %collective-permute-start.1 = (bf16[15,128]{1,0:T(8,128)(2,1)S(1)}, bf16[15,128]{1,0:T(8,128)(2,1)S(1)}, u32[]{:S(2)}, u32[]{:S(2)}) collective-permute-start(bf16[15,128]{1,0:T(8,128)(2,1)S(1)} %get-tuple-element.8), channel_id=1, source_target_pairs={{8,0},{16,8},{24,16},{32,24},{40,32},{48,40},{56,48},{64,56},{72,6... | collective-permute-start | bytes 11528 | tf_op jit(solution)/shard_map/ppermute | solution.py:17
Sparse Core Ops, SparseCore 0:
  257.7 34.3 all-gather.2
  307.7 38.4 reduce-scatter.1
